TPU v7x, 32 devices: a whole 2x2x4 slice. The times are simulated.
32 devices in a mesh: gx: 8 (over z, core), gy: 4 (over y, x).
Axes of the slice: x: 2, y: 2, z: 4, core: 2. Of those that a mesh axis runs over, the one named last changes fastest.
Arguments:
- rhs_field: float32 [128, 64, 128], P('gx', 'gy'), may hold values from -10 to 10
- diag_blocks: bfloat16 [128, 64, 128, 128], P('gx', 'gy'), may hold values from -1 to 4, as said below
- face_lift: bfloat16 [4, 128, 128], replicated, may hold values from -0.5 to 0.5
- face_state: int32 [128, 64, 4], P('gx', 'gy'), may hold values from 0 to 2
- restrict_basis: float32 [128, 8], replicated, may hold values from -0.5 to 0.5
- coarse_inverse: float32 [128, 64, 8, 8], P('gx', 'gy'), may hold values from -0.4 to 1.2
Outputs:
- solution_field: float32 [128, 64, 128], P('gx', 'gy')
- hessenberg: float32 [3, 2], replicated
Inputs may be any that keep to these rules, and one draw needn't show every extreme that they name: `diag_blocks`: each block has diagonal entries between 2 and 4 and small off-diagonal entries.
All inputs are finite; a program needn't handle non-finite values.
Results may differ from a plain program's by a relative error of at most 0.0023.
Values may be sent and summed in bfloat16 or wider, within the bound.
A program may use at most 64 MiB of HBM per device.

v0:
```python
import jax
import jax.numpy as jnp
from jax import lax
from jax.sharding import PartitionSpec as P


def padded_2(block, sides, width):
    for axis, dim in sides:
        count = lax.axis_size(axis)
        forward = [(i, i + 1) for i in range(count - 1)]
        backward = [(target, source) for source, target in forward]
        low = lax.ppermute(
            lax.slice_in_dim(block, block.shape[dim] - width, None, axis=dim), axis, forward
        )
        high = lax.ppermute(lax.slice_in_dim(block, 0, width, axis=dim), axis, backward)
        block = jnp.concatenate([low, block, high], axis=dim)
    return block


def apply_operator(field, diag_blocks, face_lift, face_state):
    rounded = field.astype(jnp.bfloat16)
    local_part = jnp.einsum(
        "ija,ijab->ijb", rounded, diag_blocks, preferred_element_type=jnp.float32
    )
    padded = padded_2(rounded, (("gx", 0), ("gy", 1)), 1)
    neighbours = [padded[:-2, 1:-1], padded[2:, 1:-1], padded[1:-1, :-2], padded[1:-1, 2:]]
    zero_block = jnp.zeros_like(rounded)
    selected = []
    for face in range(4):
        state = face_state[:, :, face][:, :, None]
        other = neighbours[face]
        selected.append(
            jnp.where(state == 1, other, jnp.where(state == 2, other[:, :, ::-1], zero_block))
        )
    stacked = jnp.concatenate(selected, axis=-1)
    width = rounded.shape[2]
    lifted = jnp.dot(
        stacked.reshape(-1, 4 * width),
        face_lift.reshape(4 * width, width),
        preferred_element_type=jnp.float32,
    )
    return local_part + lifted.reshape(field.shape)


def coarse_correct(field, restrict_basis, coarse_inverse):
    high = lax.Precision.HIGHEST
    coarse = jnp.einsum("ija,ak->ijk", field, restrict_basis, precision=high)
    rows_y = coarse.shape[1]
    column = lax.all_gather(coarse, "gy", axis=1, tiled=True)
    centred = column - jnp.mean(column, axis=1, keepdims=True)
    padded = jnp.pad(centred, ((0, 0), (1, 1), (0, 0)))
    smoothed_all = centred + 0.25 * (padded[:, :-2] + padded[:, 2:])
    start = lax.axis_index("gy") * rows_y
    smoothed = lax.dynamic_slice_in_dim(smoothed_all, start, rows_y, 1)
    solved = jnp.einsum("ijk,ijkl->ijl", smoothed, coarse_inverse, precision=high)
    return field + jnp.einsum("ijl,al->ija", solved, restrict_basis, precision=high)


def least_squares(start_len, hess):
    first = jnp.sqrt(hess[0, 0] ** 2 + hess[1, 0] ** 2)
    cos_one = hess[0, 0] / first
    sin_one = hess[1, 0] / first
    upper = cos_one * hess[0, 1] + sin_one * hess[1, 1]
    lower = -sin_one * hess[0, 1] + cos_one * hess[1, 1]
    second = jnp.sqrt(lower**2 + hess[2, 1] ** 2)
    cos_two = lower / second
    coef_two = cos_two * (-sin_one * start_len) / second
    coef_one = (cos_one * start_len - upper * coef_two) / first
    return (coef_one, coef_two)


def body(rhs_field, diag_blocks, face_lift, face_state, restrict_basis, coarse_inverse):
    start_len = jnp.sqrt(lax.psum(jnp.sum(rhs_field * rhs_field), ("gx", "gy")))
    basis = [rhs_field / start_len]
    precon = []
    hess = jnp.zeros((3, 2), jnp.float32)
    for step in range(2):
        precond = coarse_correct(basis[step], restrict_basis, coarse_inverse)
        precon.append(precond)
        image = apply_operator(precond, diag_blocks, face_lift, face_state)
        partial_dots = jnp.stack([jnp.sum(vector * image) for vector in basis])
        coeffs = lax.psum(partial_dots, ("gx", "gy"))
        for index in range(step + 1):
            image = image - coeffs[index] * basis[index]
        length = jnp.sqrt(lax.psum(jnp.sum(image * image), ("gx", "gy")))
        for index in range(step + 1):
            hess = hess.at[index, step].set(coeffs[index])
        hess = hess.at[step + 1, step].set(length)
        if step == 0:
            basis.append(image / length)
    coef_one, coef_two = least_squares(start_len, hess)
    return (coef_one * precon[0] + coef_two * precon[1], hess)


def solution(mesh):
    in_specs = (
        P("gx", "gy", None),
        P("gx", "gy", None, None),
        P(),
        P("gx", "gy", None),
        P(),
        P("gx", "gy", None, None),
    )
    out_specs = (P("gx", "gy", None), P())
    return jax.shard_map(body, mesh=mesh, in_specs=in_specs, out_specs=out_specs, check_vma=False)
```

profile of v0, /device:TPU:0, one launch (start us, length us, event | category | flops | bytes accessed | tf_op | source)
XLA Modules:
  0.0 293.5 jit_solution(4230740229205972593)
XLA Ops:
  0.6 1.6 multiply_reduce_fusion.7
  2.2 42.2 %psum.35 = f32[]{:T(128)} all-reduce(f32[]{:T(128)} %multiply_reduce_fusion.7), channel_id=1, replica_groups=mesh['gx'=8,'gy'=4] {'gx','gy'}, use_global_device_ids=true, to_apply=%region_1.0 | all-reduce | flops 1 | bytes 8 | tf_op jit(solution)/shard_map/psum | solution.py:73
  46.0 1.7 fusion.20
  47.7 10.3 %all_gather.6 = f32[16,64,8]{0,2,1:T(8,128)S(1)} all-gather(f32[16,16,8]{0,2,1:T(8,128)S(1)} %fusion.20), channel_id=1, replica_groups=mesh['gx'=8,'gy'=4] {'gy'}, dimensions={1}, use_global_device_ids=true | all-gather | bytes 40960 | tf_op jit(solution)/shard_map/all_gather | solution.py:49
  60.5 1.3 collective-permute-start
  61.8 1.3 collective-permute-start.1
  64.1 5.7 %fusion.18 = f32[16,16,1,128]{3,2,1,0:T(1,128)S(1)} fusion(bf16[16,16,128,128]{3,2,1,0:T(8,128)(2,1)} %param.17, bf16[16,16,128,1]{2,1,0,3:T(8,128)(2,1)S(1)} %bitcast.67), kind=kOutput, calls=%fused_computation.28 | convolution fusion | flops 8388608 | bytes 8585216 | tf_op jit(solution)/shard_map/ija,ijab->ijb/dot_general | solution.py:22
  69.9 2.5 collective-permute-start.2
  72.4 1.3 collective-permute-start.3
  73.7 4.2 %collective-permute-done.3 = bf16[18,1,128]{2,1,0:T(2,128)(2,1)S(1)} collective-permute-done((bf16[18,1,128]{2,1,0:T(2,128)(2,1)S(1)}, bf16[18,1,128]{2,1,0:T(2,128)(2,1)S(1)}, u32[]{:S(2)}, u32[]{:S(2)}) %collective-permute-start.3) | collective-permute-done | bytes 4640 | tf_op jit(solution)/shard_map/ppermute | solution.py:15
  79.7 42.8 %psum.36 = f32[1]{0:T(128)} all-reduce(f32[1]{0:T(128)} %bitcast.14), channel_id=1, replica_groups=mesh['gx'=8,'gy'=4] {'gx','gy'}, use_global_device_ids=true, to_apply=%region_4.5 | all-reduce | flops 1 | bytes 8 | tf_op jit(solution)/shard_map/psum | solution.py:82
  123.8 40.7 %psum.37 = f32[]{:T(128)} all-reduce(f32[]{:T(128)} %multiply_reduce_fusion.5), channel_id=1, replica_groups=mesh['gx'=8,'gy'=4] {'gx','gy'}, use_global_device_ids=true, to_apply=%region_6.7 | all-reduce | flops 1 | bytes 8 | tf_op jit(solution)/shard_map/psum | solution.py:85
  166.9 10.3 %all_gather.7 = f32[16,64,8]{0,2,1:T(8,128)S(1)} all-gather(f32[16,16,8]{0,2,1:T(8,128)S(1)} %fusion.16), channel_id=1, replica_groups=mesh['gx'=8,'gy'=4] {'gy'}, dimensions={1}, use_global_device_ids=true | all-gather | bytes 40960 | tf_op jit(solution)/shard_map/all_gather | solution.py:49
  177.9 1.3 collective-permute-start.4
  179.2 1.3 collective-permute-start.5
  181.2 2.9 collective-permute-done.5
  184.1 2.0 collective-permute-start.6
  186.2 1.3 collective-permute-start.7
  187.5 5.7 %fusion.14 = f32[16,16,1,128]{3,2,1,0:T(1,128)S(1)} fusion(bf16[16,16,128,128]{3,2,1,0:T(8,128)(2,1)} %param.17, bf16[16,16,128,1]{2,1,0,3:T(8,128)(2,1)S(1)} %bitcast.68), kind=kOutput, calls=%fused_computation.24 | convolution fusion | flops 8388608 | bytes 8585216 | tf_op jit(solution)/shard_map/ija,ijab->ijb/dot_general | solution.py:22
  195.1 1.3 pad_maximum_fusion.22
  197.1 42.6 %psum.38 = f32[2]{0:T(128)S(1)} all-reduce(f32[2]{0:T(128)S(1)} %pad_maximum_fusion.22), channel_id=1, replica_groups=mesh['gx'=8,'gy'=4] {'gx','gy'}, use_global_device_ids=true, to_apply=%region_10.11 | all-reduce | flops 2 | bytes 16 | tf_op jit(solution)/shard_map/psum | solution.py:82
  240.3 2.0 multiply_reduce_fusion.2
  242.3 39.8 %psum.39 = f32[]{:T(128)} all-reduce(f32[]{:T(128)} %multiply_reduce_fusion.2), channel_id=1, replica_groups=mesh['gx'=8,'gy'=4] {'gx','gy'}, use_global_device_ids=true, to_apply=%region_12.13 | all-reduce | flops 1 | bytes 8 | tf_op jit(solution)/shard_map/psum | solution.py:85
  282.8 1.9 scatter.20
  (72 shorter events, 16.1 us)
Async XLA Ops:
  0.6 78.2 %copy-start = (bf16[4,128,128]{2,1,0:T(8,128)(2,1)S(1)}, bf16[4,128,128]{2,1,0:T(8,128)(2,1)}, u32[]{:S(2)}) copy-start(bf16[4,128,128]{2,1,0:T(8,128)(2,1)} %param.18) | copy-start | bytes 393220
  60.5 9.3 %collective-permute-start = (bf16[1,16,128]{2,1,0:T(8,128)(2,1)S(1)}, bf16[1,16,128]{2,1,0:T(8,128)(2,1)S(1)}, u32[]{:S(2)}, u32[]{:S(2)}) collective-permute-start(bf16[1,16,128]{2,1,0:T(8,128)(2,1)S(1)} %get-tuple-element.82), channel_id=1, source_target_pairs={{0,4},{4,8},{8,12},{12,16},{16,20},{20,24},{24,28},{1,5},{5,9},{9,... | collective-permute-start | bytes 12296 | tf_op jit(solution)/shard_map/ppermute | solution.py:12
  61.8 8.1 %collective-permute-start.1 = (bf16[1,16,128]{2,1,0:T(8,128)(2,1)S(1)}, bf16[1,16,128]{2,1,0:T(8,128)(2,1)S(1)}, u32[]{:S(2)}, u32[]{:S(2)}) collective-permute-start(bf16[1,16,128]{2,1,0:T(8,128)(2,1)S(1)} %get-tuple-element.83), channel_id=1, source_target_pairs={{4,0},{8,4},{12,8},{16,12},{20,16},{24,20},{28,24},{5,1},{9,5},{13... | collective-permute-start | bytes 12296 | tf_op jit(solution)/shard_map/ppermute | solution.py:15
  64.1 58.4 %copy-start.1 = (f32[16,16,128]{2,1,0:T(8,128)S(1)}, f32[16,16,128]{2,1,0:T(8,128)}, u32[]{:S(2)}) copy-start(f32[16,16,128]{2,1,0:T(8,128)} %param.16) | copy-start | bytes 393220
  64.1 101.7 %copy-start.3 = (f32[128,8]{0,1:T(8,128)S(1)}, f32[128,8]{0,1:T(8,128)}, u32[]{:S(2)}) copy-start(f32[128,8]{0,1:T(8,128)} %param.20) | copy-start | bytes 12292
  64.1 113.3 %copy-start.2 = (f32[16,16,8,8]{1,3,2,0:T(8,128)S(1)}, f32[16,16,8,8]{1,3,2,0:T(8,128)}, u32[]{:S(2)}) copy-start(f32[16,16,8,8]{1,3,2,0:T(8,128)} %param.21) | copy-start | bytes 196612
  69.9 3.8 %collective-permute-start.2 = (bf16[18,1,128]{2,1,0:T(2,128)(2,1)S(1)}, bf16[18,1,128]{2,1,0:T(2,128)(2,1)S(1)}, u32[]{:S(2)}, u32[]{:S(2)}) collective-permute-start(bf16[18,1,128]{2,1,0:T(2,128)(2,1)S(1)} %get-tuple-element.74), channel_id=1, source_target_pairs={{0,1},{1,2},{2,3},{4,5},{5,6},{6,7},{8,9},{9,10},{10,11},{12,13},{... | collective-permute-start | bytes 13832 | tf_op jit(solution)/shard_map/ppermute | solution.py:12
  72.4 5.6 %collective-permute-start.3 = (bf16[18,1,128]{2,1,0:T(2,128)(2,1)S(1)}, bf16[18,1,128]{2,1,0:T(2,128)(2,1)S(1)}, u32[]{:S(2)}, u32[]{:S(2)}) collective-permute-start(bf16[18,1,128]{2,1,0:T(2,128)(2,1)S(1)} %get-tuple-element.75), channel_id=1, source_target_pairs={{1,0},{2,1},{3,2},{5,4},{6,5},{7,6},{9,8},{10,9},{11,10},{13,12},{... | collective-permute-start | bytes 13832 | tf_op jit(solution)/shard_map/ppermute | solution.py:15
  177.9 3.3 %collective-permute-start.4 = (bf16[1,16,128]{2,1,0:T(8,128)(2,1)S(1)}, bf16[1,16,128]{2,1,0:T(8,128)(2,1)S(1)}, u32[]{:S(2)}, u32[]{:S(2)}) collective-permute-start(bf16[1,16,128]{2,1,0:T(8,128)(2,1)S(1)} %get-tuple-element.80), channel_id=1, source_target_pairs={{0,4},{4,8},{8,12},{12,16},{16,20},{20,24},{24,28},{1,5},{5,9},{9,... | collective-permute-start | bytes 12296 | tf_op jit(solution)/shard_map/ppermute | solution.py:12
  179.2 4.9 %collective-permute-start.5 = (bf16[1,16,128]{2,1,0:T(8,128)(2,1)S(1)}, bf16[1,16,128]{2,1,0:T(8,128)(2,1)S(1)}, u32[]{:S(2)}, u32[]{:S(2)}) collective-permute-start(bf16[1,16,128]{2,1,0:T(8,128)(2,1)S(1)} %get-tuple-element.81), channel_id=1, source_target_pairs={{4,0},{8,4},{12,8},{16,12},{20,16},{24,20},{28,24},{5,1},{9,5},{13... | collective-permute-start | bytes 12296 | tf_op jit(solution)/shard_map/ppermute | solution.py:15
  184.1 9.0 %collective-permute-start.6 = (bf16[18,1,128]{2,1,0:T(2,128)(2,1)S(1)}, bf16[18,1,128]{2,1,0:T(2,128)(2,1)S(1)}, u32[]{:S(2)}, u32[]{:S(2)}) collective-permute-start(bf16[18,1,128]{2,1,0:T(2,128)(2,1)S(1)} %get-tuple-element.70), channel_id=1, source_target_pairs={{0,1},{1,2},{2,3},{4,5},{5,6},{6,7},{8,9},{9,10},{10,11},{12,13},{... | collective-permute-start | bytes 13832 | tf_op jit(solution)/shard_map/ppermute | solution.py:12
  186.2 7.0 %collective-permute-start.7 = (bf16[18,1,128]{2,1,0:T(2,128)(2,1)S(1)}, bf16[18,1,128]{2,1,0:T(2,128)(2,1)S(1)}, u32[]{:S(2)}, u32[]{:S(2)}) collective-permute-start(bf16[18,1,128]{2,1,0:T(2,128)(2,1)S(1)} %get-tuple-element.71), channel_id=1, source_target_pairs={{1,0},{2,1},{3,2},{5,4},{6,5},{7,6},{9,8},{10,9},{11,10},{13,12},{... | collective-permute-start | bytes 13832 | tf_op jit(solution)/shard_map/ppermute | solution.py:15
  285.6 7.9 %copy-start.4 = (f32[3,2]{0,1:T(2,128)}, f32[3,2]{0,1:T(2,128)S(1)}, u32[]{:S(2)}) copy-start(f32[3,2]{0,1:T(2,128)S(1)} %scatter.24) | copy-start | bytes 76
where the time goes:
time: 295 us; the launch traced here: 293 us
  blocking collectives  228 us (77%)
  matrix products  17.3 us (6%)
  starting transfers between devices  12.2 us (4%)
  other arithmetic  11 us (4%)
  between operations  9.67 us (3%)
  local copies, waits for them, and re-layouts  7.55 us (3%)
  waiting for transfers between devices  7.18 us (2%)
    psum x2, blocking collectives, body(): coeffs = lax.psum(partial_dots, ('gx', 'gy'))  85.4 us
    psum x2, blocking collectives, body(): length = jnp.sqrt(lax.psum(jnp.sum(image * image), ('gx', 'gy')))  80.4 us
    psum x1, blocking collectives, body(): start_len = jnp.sqrt(lax.psum(jnp.sum(rhs_field * rhs_field), ('gx', 'gy')))  42.2 us
    all_gather x2, blocking collectives, coarse_correct(): column = lax.all_gather(coarse, 'gy', axis=1, tiled=True)  20.6 us
    dot_general x2, matrix products, apply_operator(): jnp.einsum('ija,ijab->ijb', rounded, diag_blocks, preferred_element_type=...  11.4 us
    ppermute x4, waiting for transfers between devices, padded_2(): lax.ppermute(lax.slice_in_dim(block, 0, width, axis=dim), axis, backward)  7.11 us
    ppermute x4, starting transfers between devices, padded_2(): lax.ppermute(lax.slice_in_dim(block, block.shape[dim] - width, None, axis...  7.05 us
  transfers between devices with their start and end apart: 8, of which 2 were waited for; matrix products, arithmetic and copies ran while one was open for 4% of the time, Pallas kernels for 0%

commit v1 on v0

v1 whole, which is shorter than its diff:
```python
import functools
import jax
import jax.numpy as jnp
from jax import lax
from jax.experimental import pallas as pl
from jax.experimental.pallas import tpu as pltpu
from jax.sharding import PartitionSpec as P

MESH = pl.DeviceIdType.MESH
F32 = jnp.float32
BF16 = jnp.bfloat16


def hdot(a, b, dims=(((1,), (0,)), ((), ()))):
    return lax.dot_general(a, b, dims, precision=lax.Precision.HIGHEST, preferred_element_type=F32)


def total(x):
    return jnp.sum(jnp.sum(x, axis=0, keepdims=True), axis=1, keepdims=True)


def safe_div(a, b):
    return jnp.where(b > 0, a / jnp.where(b > 0, b, 1.0), 0.0)


def iota(shape, dim):
    return lax.broadcasted_iota(jnp.int32, shape, dim)


def kernel(nx, ny, ti, tj, n, kc, rhs, diag, lift, state, basis, cinv, out, hess_out,
           dvm, wts, masks, cext, wbuf, sends, halos, csend, chalo, msgs,
           dsem, ssem, rsem, msend, mrecv):
    gx = lax.axis_index("gx")
    gy = lax.axis_index("gy")
    me = gx * ny + gy
    count = nx * ny
    elems = ti * tj
    kk = kc * kc

    dcopies = [pltpu.make_async_copy(diag.at[q], dvm.at[q], dsem.at[q]) for q in range(ti)]
    for c in dcopies:
        c.start()

    barrier = pltpu.get_barrier_semaphore()

    def greet(k, carry):
        t = lax.rem(me + k, count)
        pl.semaphore_signal(barrier, inc=1, device_id=(t // ny, lax.rem(t, ny)), device_id_type=MESH)
        return carry

    lax.fori_loop(1, count, greet, 0)

    has_n, has_s, has_w, has_e = gx > 0, gx < nx - 1, gy > 0, gy < ny - 1
    h = 2 * ti + 2 * tj
    o_n, o_s, o_w, o_e = 0, tj, 2 * tj, 2 * tj + 2 * ti
    o_nw = 2 * tj + 4 * ti
    o_ne, o_sw, o_se = o_nw + 8, o_nw + 16, o_nw + 24
    hrows = o_nw + 32
    routes = [
        (has_n, (gx - 1, gy), o_n, o_s, tj),
        (has_s, (gx + 1, gy), o_s, o_n, tj),
        (has_w, (gx, gy - 1), o_w, o_e, 2 * ti),
        (has_e, (gx, gy + 1), o_e, o_w, 2 * ti),
        (jnp.logical_and(has_n, has_w), (gx - 1, gy - 1), o_nw, o_se, 8),
        (jnp.logical_and(has_n, has_e), (gx - 1, gy + 1), o_ne, o_sw, 8),
        (jnp.logical_and(has_s, has_w), (gx + 1, gy - 1), o_sw, o_ne, 8),
        (jnp.logical_and(has_s, has_e), (gx + 1, gy + 1), o_se, o_nw, 8),
    ]
    croutes = [
        (has_n, (gx - 1, gy), 0, tj, tj),
        (has_s, (gx + 1, gy), tj, 0, tj),
        (has_w, (gx, gy - 1), 2 * tj, 2 * tj + ti, ti),
        (has_e, (gx, gy + 1), 2 * tj + ti, 2 * tj, ti),
    ]
    opposite = [1, 0, 3, 2, 7, 6, 5, 4]

    def rim_copies(g):
        return [(ok, pltpu.make_async_remote_copy(
            src_ref=sends.at[g, pl.ds(src, rows)], dst_ref=halos.at[g, pl.ds(dst, rows)],
            send_sem=ssem.at[g, d], recv_sem=rsem.at[g, opposite[d]],
            device_id=dev, device_id_type=MESH)) for d, (ok, dev, src, dst, rows) in enumerate(routes)]

    def coarse_copies():
        return [(ok, pltpu.make_async_remote_copy(
            src_ref=csend.at[pl.ds(src, rows)], dst_ref=chalo.at[pl.ds(dst, rows)],
            send_sem=ssem.at[2, d], recv_sem=rsem.at[2, opposite[d]],
            device_id=dev, device_id_type=MESH)) for d, (ok, dev, src, dst, rows) in enumerate(croutes)]

    def rim_wait(g, which):
        table = routes if g < 2 else croutes
        for d, (ok, dev, src, dst, rows) in enumerate(table):
            @pl.when(ok)
            def _(d=d, dev=dev, src=src, rows=rows):
                if g < 2:
                    s, r = sends.at[g, pl.ds(src, rows)], halos.at[g, pl.ds(src, rows)]
                else:
                    s, r = csend.at[pl.ds(src, rows)], chalo.at[pl.ds(src, rows)]
                c = pltpu.make_async_remote_copy(
                    src_ref=s, dst_ref=r, send_sem=ssem.at[g, d], recv_sem=rsem.at[g, d],
                    device_id=dev, device_id_type=MESH)
                if which == "send":
                    c.wait_send()
                else:
                    c.wait_recv()

    def start_all(copies):
        for ok, c in copies:
            @pl.when(ok)
            def _(c=c):
                c.start()

    def broadcast(g):
        def one(k, carry):
            t = lax.rem(me + k, count)
            pltpu.make_async_remote_copy(
                src_ref=msgs.at[g, me], dst_ref=msgs.at[g, me], send_sem=msend.at[g], recv_sem=mrecv.at[g],
                device_id=(t // ny, lax.rem(t, ny)), device_id_type=MESH).start()
            return carry
        lax.fori_loop(1, count, one, 0)

    def bc_wait(g, which):
        part = msgs.at[g, pl.ds(0, count - 1)]
        c = pltpu.make_async_remote_copy(
            src_ref=part, dst_ref=part, send_sem=msend.at[g], recv_sem=mrecv.at[g],
            device_id=(gx, gy), device_id_type=MESH)
        if which == "send":
            c.wait_send()
        else:
            c.wait_recv()

    def fill_sends(g, ref):
        sends[g, o_n:o_n + tj] = ref[0]
        sends[g, o_s:o_s + tj] = ref[ti - 1]
        sends[g, o_w:o_w + ti] = ref[:, 0, :]
        sends[g, o_w + ti:o_w + 2 * ti] = ref[:, 1, :]
        sends[g, o_e:o_e + ti] = ref[:, tj - 1, :]
        sends[g, o_e + ti:o_e + 2 * ti] = ref[:, tj - 2, :]
        sends[g, o_nw:o_nw + 8] = jnp.broadcast_to(ref[0, 0:1, :], (8, n))
        sends[g, o_ne:o_ne + 8] = jnp.broadcast_to(ref[0, tj - 1:tj, :], (8, n))
        sends[g, o_sw:o_sw + 8] = jnp.broadcast_to(ref[ti - 1, 0:1, :], (8, n))
        sends[g, o_se:o_se + 8] = jnp.broadcast_to(ref[ti - 1, tj - 1:tj, :], (8, n))

    lane1 = iota((1, n), 1)

    def message(values):
        row = jnp.zeros((1, n), F32)
        for p, v in enumerate(values):
            row = jnp.where(lane1 == p, v, row)
        return row

    R = basis[...]
    e1 = (iota((kc, n), 1) // kc == iota((kc, n), 0)).astype(F32)
    e3 = (lax.rem(iota((kc, n), 1), kc) == iota((kc, n), 0)).astype(F32)
    e4 = (lax.rem(iota((n, kc), 0), kc) == iota((n, kc), 1)).astype(F32)
    RT = hdot(R, e3)
    pick = iota((ti, n), 1) // kc == iota((ti, n), 0)

    def packed_rowsum(f3):
        rows = hdot(jnp.sum(f3, axis=1), RT)
        return jnp.sum(jnp.where(pick, rows, 0.0), axis=0, keepdims=True)

    rhs3 = rhs[...]
    rhs2 = rhs3.reshape(elems, n)
    fill_sends(0, rhs)
    csend[0:tj] = cinv[0]
    csend[tj:2 * tj] = cinv[ti - 1]
    csend[2 * tj:2 * tj + ti] = cinv[:, 0, :]
    csend[2 * tj + ti:2 * tj + 2 * ti] = cinv[:, tj - 1, :]
    msgs[0, me, 0:1] = message([total(rhs2 * rhs2)])
    msgs[0, me, 1:2] = packed_rowsum(rhs3)

    pl.semaphore_wait(barrier, count - 1)
    broadcast(0)
    start_all(rim_copies(0))
    start_all(coarse_copies())

    RE = hdot(R, e1)
    RF = hdot(e4, R, (((1,), (1,)), ((), ())))
    G = (lax.rem(iota((n, n), 0), kc) == iota((n, n), 1) // kc).astype(F32)
    flip = (iota((n, n), 0) + iota((n, n), 1) == n - 1).astype(BF16)
    for f in range(4):
        wts[2 * f * n:(2 * f + 1) * n] = lift[f]
        wts[(2 * f + 1) * n:(2 * f + 2) * n] = jnp.dot(flip, lift[f], preferred_element_type=F32).astype(BF16)
    st = state[...]
    for f in range(4):
        col = jnp.broadcast_to(st[:, f:f + 1], (elems, n))
        masks[2 * f] = (col == 1).astype(F32)
        masks[2 * f + 1] = (col == 2).astype(F32)

    hrow = iota((hrows, 1), 0)
    n_i, s_i, w_i, e_i = [v.astype(jnp.int32) for v in (has_n, has_s, has_w, has_e)]
    valid = jnp.where(hrow < o_s, n_i, jnp.where(hrow < o_w, s_i, jnp.where(
        hrow < o_e, w_i, jnp.where(hrow < o_nw, e_i, jnp.where(
            hrow < o_ne, n_i * w_i, jnp.where(hrow < o_sw, n_i * e_i, jnp.where(
                hrow < o_se, s_i * w_i, s_i * e_i))))))) > 0

    jrow = lax.rem(iota((elems, 1), 0), tj)
    trow = iota((tj, 1), 0)

    def spread(col):
        return jnp.broadcast_to(col[:, None, :], (ti, tj, n)).reshape(elems, n)

    def left_of(x, edge):
        return jnp.where(jrow == 0, spread(edge), pltpu.roll(x, 1, 0))

    def right_of(x, edge):
        return jnp.where(jrow == tj - 1, spread(edge), pltpu.roll(x, elems - 1, 0))

    def line_sum(g, line):
        acc = msgs[g, line * ny, 1:2]
        for q in range(1, ny):
            acc = acc + msgs[g, line * ny + q, 1:2]
        return acc

    def three_lines(g):
        return (line_sum(g, gx), line_sum(g, jnp.maximum(gx - 1, 0)), line_sum(g, jnp.minimum(gx + 1, nx - 1)))

    def precondition(f_own, f_halo, lines):
        p_c, p_n, p_s = lines
        stack = jnp.concatenate([
            jnp.where(pick, jnp.broadcast_to(p_c, (ti, n)), 0.0),
            jnp.broadcast_to(jnp.where(lane1 // kc == ti - 1, p_n, 0.0), (8, n)),
            jnp.broadcast_to(jnp.where(lane1 // kc == 0, p_s, 0.0), (8, n))], axis=0)
        mean = hdot(stack, G) * (1.0 / (ny * tj))
        m_c, m_n, m_s = mean[0:ti], mean[ti:ti + 1], mean[ti + 8:ti + 9]
        c_own = hdot(f_own, RE) - spread(m_c)
        c_halo = hdot(f_halo, RE)
        m_halo = jnp.concatenate([
            jnp.broadcast_to(m_n, (tj, n)), jnp.broadcast_to(m_s, (tj, n)), m_c, m_c, m_c, m_c,
            jnp.broadcast_to(m_n, (16, n)), jnp.broadcast_to(m_s, (16, n))], axis=0)
        c_halo = jnp.where(valid, c_halo - m_halo, 0.0)
        c_w1, c_w2 = c_halo[o_w:o_w + ti], c_halo[o_w + ti:o_e]
        c_e1, c_e2 = c_halo[o_e:o_e + ti], c_halo[o_e + ti:o_nw]
        c_n, c_s = c_halo[o_n:o_n + tj], c_halo[o_s:o_s + tj]
        c3 = c_own.reshape(ti, tj, n)
        s_own = c_own + 0.25 * (left_of(c_own, c_w1) + right_of(c_own, c_e1))

        def row_smooth(x, lo, hi):
            left = jnp.where(trow == 0, lo, pltpu.roll(x, 1, 0))
            right = jnp.where(trow == tj - 1, hi, pltpu.roll(x, tj - 1, 0))
            return x + 0.25 * (left + right)
        s_n = row_smooth(c_n, c_halo[o_nw:o_nw + 1], c_halo[o_ne:o_ne + 1])
        s_s = row_smooth(c_s, c_halo[o_sw:o_sw + 1], c_halo[o_se:o_se + 1])
        s_w = c_w1 + 0.25 * (c_w2 + c3[:, 0, :])
        s_e = c_e1 + 0.25 * (c3[:, tj - 1, :] + c_e2)
        z_own = f_own + hdot(s_own * cext[0:elems], RF)
        f_rim = jnp.concatenate([f_halo[o_n:o_w], f_halo[o_w:o_w + ti], f_halo[o_e:o_e + ti]], axis=0)
        ok_rim = jnp.concatenate([valid[o_n:o_w], valid[o_w:o_w + ti], valid[o_e:o_e + ti]], axis=0)
        s_rim = jnp.concatenate([s_n, s_s, s_w, s_e], axis=0)
        z_rim = jnp.where(ok_rim, f_rim + hdot(s_rim * cext[elems:elems + h], RF), 0.0)
        return z_own, z_rim

    def operator(z, z_rim):
        nb = [
            jnp.concatenate([z_rim[0:tj], z[0:elems - tj]], axis=0),
            jnp.concatenate([z[tj:], z_rim[tj:2 * tj]], axis=0),
            left_of(z, z_rim[2 * tj:2 * tj + ti]),
            right_of(z, z_rim[2 * tj + ti:2 * tj + 2 * ti]),
        ]
        cols = []
        for f in range(4):
            cols.append((nb[f] * masks[2 * f]).astype(BF16))
            cols.append((nb[f] * masks[2 * f + 1]).astype(BF16))
        lifted = jnp.dot(jnp.concatenate(cols, axis=1), wts[...], preferred_element_type=F32)
        wbuf[...] = lifted.reshape(ti, tj, n)
        erow = iota((tj, n), 0)
        for q in range(0, ti, 2):
            a = z[q * tj:(q + 1) * tj]
            b = z[(q + 1) * tj:(q + 2) * tj]
            lhs = jnp.concatenate([jnp.concatenate(
                [jnp.where(erow == e, a, 0.0), jnp.where(erow == e, b, 0.0)], axis=0).astype(BF16)
                for e in range(tj)], axis=1)
            rhs_w = jnp.concatenate([dvm[q].reshape(tj * n, n), dvm[q + 1].reshape(tj * n, n)], axis=1)
            prod = jnp.dot(lhs, rhs_w, preferred_element_type=F32)
            wbuf[q] += prod[0:tj, 0:n]
            wbuf[q + 1] += prod[tj:2 * tj, n:2 * n]

    bc_wait(0, "recv")
    rim_wait(0, "recv")
    rim_wait(2, "recv")

    cext[0:elems] = cinv[...].reshape(elems, n)
    cext[elems:elems + h] = chalo[...]
    lens = msgs[0, :, 0, :][:, 0:1]
    start_len = jnp.sqrt(jnp.sum(lens, axis=0, keepdims=True))
    inv_len = 1.0 / start_len
    n_one = lens * inv_len * inv_len
    v1 = rhs2 * inv_len
    v1_halo = jnp.where(valid, halos[0] * inv_len, 0.0)
    lines1 = [p * inv_len for p in three_lines(0)]
    z1, z1_rim = precondition(v1, v1_halo, lines1)
    for c in dcopies:
        c.wait()
    operator(z1, z1_rim)
    fill_sends(1, wbuf)
    start_all(rim_copies(1))
    w1 = wbuf[...].reshape(elems, n)
    own_n1 = total(v1 * v1)
    dot_one = total(v1 * w1)
    p_one = safe_div(dot_one, own_n1)
    gap = w1 - p_one * v1
    msgs[1, me, 0:1] = message([dot_one, p_one, total(gap * gap), own_n1])
    msgs[1, me, 1:2] = packed_rowsum(wbuf[...])
    broadcast(1)
    bc_wait(1, "recv")
    rim_wait(1, "recv")

    X = msgs[1, :, 0, :]
    h11 = jnp.sum(X[:, 0:1], axis=0, keepdims=True)
    dev = X[:, 1:2] - h11
    h21 = jnp.sqrt(jnp.sum(X[:, 2:3] + dev * dev * X[:, 3:4], axis=0, keepdims=True))
    inv21 = 1.0 / h21
    v2 = (w1 - h11 * v1) * inv21
    v2_halo = jnp.where(valid, (halos[1] - h11 * v1_halo) * inv21, 0.0)
    lines2 = [(pw - h11 * pv) * inv21 for pw, pv in zip(three_lines(1), lines1)]
    z2, z2_rim = precondition(v2, v2_halo, lines2)
    operator(z2, z2_rim)
    w2 = wbuf[...].reshape(elems, n)
    alpha = safe_div(total(v1 * v2), own_n1)
    q2 = v2 - alpha * v1
    nq = total(q2 * q2)
    d1 = total(w2 * v1)
    d2 = total(w2 * v2)
    p1 = safe_div(d1, own_n1)
    p2 = safe_div(d2 - alpha * d1, nq)
    gap2 = w2 - p1 * v1 - p2 * q2
    msgs[2, me, 0:1] = message([d1, d2, alpha, nq, p1, p2, total(gap2 * gap2), own_n1])
    msgs[2, me, 1:2] = jnp.zeros((1, n), F32)
    broadcast(2)
    bc_wait(2, "recv")
    Y = msgs[2, :, 0, :]
    h12 = jnp.sum(Y[:, 0:1], axis=0, keepdims=True)
    h22 = jnp.sum(Y[:, 1:2], axis=0, keepdims=True)
    t1 = Y[:, 4:5] - h12 - h22 * Y[:, 2:3]
    t2 = Y[:, 5:6] - h22
    h32 = jnp.sqrt(jnp.sum(t1 * t1 * Y[:, 7:8] + t2 * t2 * Y[:, 3:4] + Y[:, 6:7], axis=0, keepdims=True))

    first = jnp.sqrt(h11 * h11 + h21 * h21)
    cos_one = h11 / first
    sin_one = h21 / first
    upper = cos_one * h12 + sin_one * h22
    lower = -sin_one * h12 + cos_one * h22
    second = jnp.sqrt(lower * lower + h32 * h32)
    cos_two = lower / second
    y2 = cos_two * (-sin_one * start_len) / second
    y1 = (cos_one * start_len - upper * y2) / first
    out[...] = (y1 * z1 + y2 * z2).reshape(ti, tj, n)
    hr, hc = iota((3, 2), 0), iota((3, 2), 1)
    hess_out[...] = jnp.where(
        hr == 0, jnp.where(hc == 0, h11, h12),
        jnp.where(hr == 1, jnp.where(hc == 0, h21, h22), jnp.where(hc == 0, 0.0, h32)))

    for g in range(3):
        bc_wait(g, "send")
        rim_wait(g, "send")


def solution(mesh):
    nx, ny = mesh.shape["gx"], mesh.shape["gy"]

    def body(rhs, diag, lift, state, basis, cinv):
        ti, tj, n = rhs.shape
        kc = basis.shape[1]
        cflat = jnp.pad(cinv.reshape(ti, tj, kc * kc), ((0, 0), (0, 0), (0, n - kc * kc)))
        sflat = state.reshape(ti * tj, 4)
        hrows = 2 * tj + 4 * ti + 32
        h = 2 * ti + 2 * tj
        vm = pl.BlockSpec(memory_space=pltpu.VMEM)
        return pl.pallas_call(
            functools.partial(kernel, nx, ny, ti, tj, n, kc),
            out_shape=(jax.ShapeDtypeStruct((ti, tj, n), F32), jax.ShapeDtypeStruct((3, 2), F32)),
            in_specs=[vm, pl.BlockSpec(memory_space=pl.ANY), vm, vm, vm, vm],
            out_specs=(vm, vm),
            scratch_shapes=[
                pltpu.VMEM((ti, tj, n, n), BF16),
                pltpu.VMEM((8 * n, n), BF16),
                pltpu.VMEM((8, ti * tj, n), F32),
                pltpu.VMEM((ti * tj + h, n), F32),
                pltpu.VMEM((ti, tj, n), F32),
                pltpu.VMEM((2, hrows, n), F32),
                pltpu.VMEM((2, hrows, n), F32),
                pltpu.VMEM((h, n), F32),
                pltpu.VMEM((h, n), F32),
                pltpu.VMEM((3, nx * ny, 2, n), F32),
                pltpu.SemaphoreType.DMA((ti,)),
                pltpu.SemaphoreType.DMA((3, 8)),
                pltpu.SemaphoreType.DMA((3, 8)),
                pltpu.SemaphoreType.DMA((3,)),
                pltpu.SemaphoreType.DMA((3,)),
            ],
            compiler_params=pltpu.CompilerParams(collective_id=0, has_side_effects=True,
                                                 vmem_limit_bytes=40 * 1024 * 1024),
        )(rhs, diag, lift, sflat, basis, cflat)

    in_specs = (P("gx", "gy", None), P("gx", "gy", None, None), P(), P("gx", "gy", None), P(),
                P("gx", "gy", None, None))
    return jax.shard_map(body, mesh=mesh, in_specs=in_specs, out_specs=(P("gx", "gy", None), P()), check_vma=False)
```

time: 295 us -> 37.1 us (0.13)
  blocking collectives: 228 us -> 0 us
  Pallas kernels: 0 us -> 26.7 us
  matrix products: 17.3 us -> 0 us
  starting transfers between devices: 12.2 us -> 0 us
  other arithmetic: 11 us -> 0 us
  between operations: 9.67 us -> 0.66 us
  waiting for transfers between devices: 7.18 us -> 0 us
    psum x5 -> x0, blocking collectives: 208 us -> none  [the longest x2 85.4 us: body(): coeffs = lax.psum(partial_dots, ('gx', 'gy'))]
    pallas_call x0 -> x1, Pallas kernels: none -> 26.7 us  [body(): pl.pallas_call(functools.partial(kernel, nx, ny, ti, tj, n, kc), out_shap...]
    all_gather x2 -> x0, blocking collectives: 20.6 us -> none  [coarse_correct(): column = lax.all_gather(coarse, 'gy', axis=1, tiled=True)]
    dot_general x8 -> x0, matrix products: 17.3 us -> none  [the longest x2 11.4 us: apply_operator(): jnp.einsum('ija,ijab->ijb', rounded, diag_blocks, preferred_element_type=...]
    ppermute x8 -> x0, starting transfers between devices: 12.2 us -> none  [the longest x4 7.05 us: padded_2(): lax.ppermute(lax.slice_in_dim(block, block.shape[dim] - width, None, axis...]
    unnamed x12 -> x9, local copies, waits for them, and re-layouts: 0.23 us -> 7.55 us
    ppermute x8 -> x0, waiting for transfers between devices: 7.18 us -> none  [the longest x4 7.11 us: padded_2(): lax.ppermute(lax.slice_in_dim(block, 0, width, axis=dim), axis, backward)]
    reduce_sum x5 -> x0, other arithmetic: 4.99 us -> none  [the longest x2 3.27 us: body(): length = jnp.sqrt(lax.psum(jnp.sum(image * image), ('gx', 'gy')))]
  transfers between devices with their start and end apart: 8 -> 0, of which waited for: 2 -> 0; matrix products, arithmetic and copies ran while one was open for 4% -> 0% of each run, Pallas kernels for 0% -> 0%
where the time goes in v1:
time: 37.1 us; the launch traced here: 36.8 us
  Pallas kernels  26.7 us (72%)
  local copies, waits for them, and re-layouts  9.43 us (25%)
  between operations  0.66 us (2%)
    pallas_call x1, Pallas kernels, body(): pl.pallas_call(functools.partial(kernel, nx, ny, ti, tj, n, kc), out_shap...  26.7 us
    unnamed x9, local copies, waits for them, and re-layouts  7.55 us
    reshape x1, local copies, waits for them, and re-layouts, body(): cinv.reshape(ti, tj, kc * kc)  1.22 us

profile of v1, /device:TPU:0, one launch (start us, length us, event | category | flops | bytes accessed | tf_op | source)
XLA Modules:
  0.0 36.8 jit_solution(286864462562171890)
XLA Ops:
  0.6 0.8 %copy.14.basis = f32[128,8]{1,0:T(8,128)S(1)} copy(f32[128,8]{0,1:T(8,128)} %param.10) | data formatting | bytes 8192 | tf_op args[4]
  1.4 0.9 %copy.12 = s32[16,16,4]{2,1,0:T(8,128)S(1)} copy(s32[16,16,4]{1,2,0:T(4,128)} %param.9) | data formatting | bytes 8192 | tf_op args[3]
  2.3 1.2 %copy.13 = f32[16,16,64]{2,1,0:T(8,128)S(1)} copy(f32[16,16,64]{1,2,0:T(8,128)} %bitcast.3) | data formatting | bytes 131072 | tf_op jit(solution)/shard_map/reshape | solution.py:364
  3.6 0.0 copy-start
  3.6 3.4 %copy-done = bf16[16,16,128,128]{3,2,1,0:T(8,128)(2,1)S(1)} copy-done((bf16[16,16,128,128]{3,2,1,0:T(8,128)(2,1)S(1)}, bf16[16,16,128,128]{3,2,1,0:T(8,128)(2,1)}, u32[]{:S(2)}) %copy-start) | copy-done | bytes 8388632
  7.0 0.0 copy-start.1
  7.0 0.9 %copy-done.1 = f32[16,16,128]{2,1,0:T(8,128)S(1)} copy-done((f32[16,16,128]{2,1,0:T(8,128)S(1)}, f32[16,16,128]{2,1,0:T(8,128)}, u32[]{:S(2)}) %copy-start.1) | copy-done | bytes 131096
  7.9 0.0 copy-start.2
  7.9 0.9 %copy-done.2 = bf16[4,128,128]{2,1,0:T(8,128)(2,1)S(1)} copy-done((bf16[4,128,128]{2,1,0:T(8,128)(2,1)S(1)}, bf16[4,128,128]{2,1,0:T(8,128)(2,1)}, u32[]{:S(2)}) %copy-start.2) | copy-done | bytes 131096
  8.8 26.7 %shard_map.77 = (f32[16,16,128]{2,1,0:T(8,128)S(1)}, f32[3,2]{1,0:T(4,128)S(1)}) custom-call(f32[16,16,128]{2,1,0:T(8,128)S(1)} %copy-done.1, bf16[16,16,128,128]{3,2,1,0:T(8,128)(2,1)S(1)} %copy-done, bf16[4,128,128]{2,1,0:T(8,128)(2,1)S(1)} %copy-done.2, s32[256,4]{1,0:T(8,128)S(1)} %bitcast.2, f32[128,8]{1,0:T(8,128)S(1)} %copy.14.basis, ...), custom_call_target="tpu_custom_call" | custom-call | tf_op jit(solution)/shard_map/pallas_call | solution.py:369
  35.5 0.6 %copy.15 = f32[3,2]{0,1:T(2,128)} copy(f32[3,2]{1,0:T(4,128)S(1)} %get-tuple-element.5) | data formatting | bytes 48 | tf_op jit(solution)/shard_map/pallas_call | solution.py:369
  36.1 0.7 %copy.17 = f32[16,16,128]{2,1,0:T(8,128)} copy(f32[16,16,128]{2,1,0:T(8,128)S(1)} %get-tuple-element.8) | data formatting | bytes 262144
  (1 shorter events, 0.0 us)
Async XLA Ops:
  3.6 3.4 %copy-start = (bf16[16,16,128,128]{3,2,1,0:T(8,128)(2,1)S(1)}, bf16[16,16,128,128]{3,2,1,0:T(8,128)(2,1)}, u32[]{:S(2)}) copy-start(bf16[16,16,128,128]{3,2,1,0:T(8,128)(2,1)} %diag.1) | copy-start | bytes 25165828
  7.0 0.9 %copy-start.1 = (f32[16,16,128]{2,1,0:T(8,128)S(1)}, f32[16,16,128]{2,1,0:T(8,128)}, u32[]{:S(2)}) copy-start(f32[16,16,128]{2,1,0:T(8,128)} %rhs.1) | copy-start | bytes 393220
  7.9 0.9 %copy-start.2 = (bf16[4,128,128]{2,1,0:T(8,128)(2,1)S(1)}, bf16[4,128,128]{2,1,0:T(8,128)(2,1)}, u32[]{:S(2)}) copy-start(bf16[4,128,128]{2,1,0:T(8,128)(2,1)} %lift.1) | copy-start | bytes 393220

commit v2 on v1

--- a/solution.py
+++ b/solution.py
@@ -27,9 +27,10 @@
     return lax.broadcasted_iota(jnp.int32, shape, dim)
 
 
-def kernel(nx, ny, ti, tj, n, kc, rhs, diag, lift, state, basis, cinv, out, hess_out,
+def kernel(nx, ny, ti, tj, n, kc, rhs_h, diag, lift_h, state_h, basis_h, cinv_h, out, hess_out,
+           rhs, lift, state, basis, cinv,
            dvm, wts, masks, cext, wbuf, sends, halos, csend, chalo, msgs,
-           dsem, ssem, rsem, msend, mrecv):
+           isem, dsem, ssem, rsem, msend, mrecv):
     gx = lax.axis_index("gx")
     gy = lax.axis_index("gy")
     me = gx * ny + gy
@@ -37,6 +38,10 @@
     elems = ti * tj
     kk = kc * kc
 
+    loads = [pltpu.make_async_copy(a, b, isem.at[q]) for q, (a, b) in enumerate(
+        ((rhs_h, rhs), (basis_h, basis), (cinv_h, cinv), (state_h, state), (lift_h, lift)))]
+    for c in loads:
+        c.start()
     dcopies = [pltpu.make_async_copy(diag.at[q], dvm.at[q], dsem.at[q]) for q in range(ti)]
     for c in dcopies:
         c.start()
@@ -148,12 +153,14 @@
             row = jnp.where(lane1 == p, v, row)
         return row
 
-    R = basis[...]
     e1 = (iota((kc, n), 1) // kc == iota((kc, n), 0)).astype(F32)
     e3 = (lax.rem(iota((kc, n), 1), kc) == iota((kc, n), 0)).astype(F32)
-    e4 = (lax.rem(iota((n, kc), 0), kc) == iota((n, kc), 1)).astype(F32)
-    RT = hdot(R, e3)
     pick = iota((ti, n), 1) // kc == iota((ti, n), 0)
+    loads[0].wait()
+    loads[1].wait()
+    Rt = basis[...]
+    over_first = (((0,), (0,)), ((), ()))
+    RT = hdot(Rt, e3, over_first)
 
     def packed_rowsum(f3):
         rows = hdot(jnp.sum(f3, axis=1), RT)
@@ -162,30 +169,42 @@
     rhs3 = rhs[...]
     rhs2 = rhs3.reshape(elems, n)
     fill_sends(0, rhs)
-    csend[0:tj] = cinv[0]
-    csend[tj:2 * tj] = cinv[ti - 1]
-    csend[2 * tj:2 * tj + ti] = cinv[:, 0, :]
-    csend[2 * tj + ti:2 * tj + 2 * ti] = cinv[:, tj - 1, :]
     msgs[0, me, 0:1] = message([total(rhs2 * rhs2)])
     msgs[0, me, 1:2] = packed_rowsum(rhs3)
 
     pl.semaphore_wait(barrier, count - 1)
     broadcast(0)
     start_all(rim_copies(0))
+    loads[2].wait()
+    cext[...] = jnp.zeros_like(cext)
+    eye = (iota((tj, tj), 0) == iota((tj, tj), 1)).astype(F32)
+    for q in range(ti):
+        cext[q * tj:(q + 1) * tj, 0:kk] = hdot(eye, cinv[q], (((1,), (1,)), ((), ())))
+    c3d = cext[0:elems].reshape(ti, tj, n)
+    csend[0:tj] = c3d[0]
+    csend[tj:2 * tj] = c3d[ti - 1]
+    csend[2 * tj:2 * tj + ti] = c3d[:, 0, :]
+    csend[2 * tj + ti:2 * tj + 2 * ti] = c3d[:, tj - 1, :]
     start_all(coarse_copies())
 
-    RE = hdot(R, e1)
-    RF = hdot(e4, R, (((1,), (1,)), ((), ())))
+    RE = hdot(Rt, e1, over_first)
+    e4 = (lax.rem(iota((n, kc), 0), kc) == iota((n, kc), 1)).astype(F32)
+    RF = hdot(e4, Rt)
     G = (lax.rem(iota((n, n), 0), kc) == iota((n, n), 1) // kc).astype(F32)
     flip = (iota((n, n), 0) + iota((n, n), 1) == n - 1).astype(BF16)
+    loads[4].wait()
     for f in range(4):
         wts[2 * f * n:(2 * f + 1) * n] = lift[f]
         wts[(2 * f + 1) * n:(2 * f + 2) * n] = jnp.dot(flip, lift[f], preferred_element_type=F32).astype(BF16)
-    st = state[...]
+    loads[3].wait()
+    own_j = lax.rem(iota((elems, tj), 0), tj) == iota((elems, tj), 1)
+    ones = jnp.ones((tj, n), BF16)
     for f in range(4):
-        col = jnp.broadcast_to(st[:, f:f + 1], (elems, n))
-        masks[2 * f] = (col == 1).astype(F32)
-        masks[2 * f + 1] = (col == 2).astype(F32)
+        rows = state[:, f, :].astype(F32)
+        wide = jnp.broadcast_to(rows[:, None, :], (ti, tj, tj)).reshape(elems, tj)
+        col = jnp.dot(jnp.where(own_j, wide, 0.0).astype(BF16), ones, preferred_element_type=F32)
+        masks[2 * f] = (col == 1.0).astype(F32)
+        masks[2 * f + 1] = (col == 2.0).astype(F32)
 
     hrow = iota((hrows, 1), 0)
     n_i, s_i, w_i, e_i = [v.astype(jnp.int32) for v in (has_n, has_s, has_w, has_e)]
@@ -279,7 +298,6 @@
     rim_wait(0, "recv")
     rim_wait(2, "recv")
 
-    cext[0:elems] = cinv[...].reshape(elems, n)
     cext[elems:elems + h] = chalo[...]
     lens = msgs[0, :, 0, :][:, 0:1]
     start_len = jnp.sqrt(jnp.sum(lens, axis=0, keepdims=True))
@@ -345,7 +363,7 @@
     y2 = cos_two * (-sin_one * start_len) / second
     y1 = (cos_one * start_len - upper * y2) / first
     out[...] = (y1 * z1 + y2 * z2).reshape(ti, tj, n)
-    hr, hc = iota((3, 2), 0), iota((3, 2), 1)
+    hr, hc = iota((2, 3), 1), iota((2, 3), 0)
     hess_out[...] = jnp.where(
         hr == 0, jnp.where(hc == 0, h11, h12),
         jnp.where(hr == 1, jnp.where(hc == 0, h21, h22), jnp.where(hc == 0, 0.0, h32)))
@@ -361,17 +379,23 @@
     def body(rhs, diag, lift, state, basis, cinv):
         ti, tj, n = rhs.shape
         kc = basis.shape[1]
-        cflat = jnp.pad(cinv.reshape(ti, tj, kc * kc), ((0, 0), (0, 0), (0, n - kc * kc)))
-        sflat = state.reshape(ti * tj, 4)
+        cflat = jnp.transpose(cinv, (0, 2, 3, 1)).reshape(ti, kc * kc, tj)
+        sflat = jnp.transpose(state, (0, 2, 1))
         hrows = 2 * tj + 4 * ti + 32
         h = 2 * ti + 2 * tj
         vm = pl.BlockSpec(memory_space=pltpu.VMEM)
-        return pl.pallas_call(
+        hbm = pl.BlockSpec(memory_space=pltpu.HBM)
+        sol, hess = pl.pallas_call(
             functools.partial(kernel, nx, ny, ti, tj, n, kc),
-            out_shape=(jax.ShapeDtypeStruct((ti, tj, n), F32), jax.ShapeDtypeStruct((3, 2), F32)),
-            in_specs=[vm, pl.BlockSpec(memory_space=pl.ANY), vm, vm, vm, vm],
+            out_shape=(jax.ShapeDtypeStruct((ti, tj, n), F32), jax.ShapeDtypeStruct((2, 3), F32)),
+            in_specs=[hbm] * 6,
             out_specs=(vm, vm),
             scratch_shapes=[
+                pltpu.VMEM((ti, tj, n), F32),
+                pltpu.VMEM((4, n, n), BF16),
+                pltpu.VMEM((ti, 4, tj), jnp.int32),
+                pltpu.VMEM((kc, n), F32),
+                pltpu.VMEM((ti, kc * kc, tj), F32),
                 pltpu.VMEM((ti, tj, n, n), BF16),
                 pltpu.VMEM((8 * n, n), BF16),
                 pltpu.VMEM((8, ti * tj, n), F32),
@@ -382,6 +406,7 @@
                 pltpu.VMEM((h, n), F32),
                 pltpu.VMEM((h, n), F32),
                 pltpu.VMEM((3, nx * ny, 2, n), F32),
+                pltpu.SemaphoreType.DMA((5,)),
                 pltpu.SemaphoreType.DMA((ti,)),
                 pltpu.SemaphoreType.DMA((3, 8)),
                 pltpu.SemaphoreType.DMA((3, 8)),
@@ -389,8 +414,9 @@
                 pltpu.SemaphoreType.DMA((3,)),
             ],
             compiler_params=pltpu.CompilerParams(collective_id=0, has_side_effects=True,
-                                                 vmem_limit_bytes=40 * 1024 * 1024),
-        )(rhs, diag, lift, sflat, basis, cflat)
+                                                 vmem_limit_bytes=60 * 1024 * 1024),
+        )(rhs, diag, lift, sflat, basis.T, cflat)
+        return sol, hess.T
 
     in_specs = (P("gx", "gy", None), P("gx", "gy", None, None), P(), P("gx", "gy", None), P(),
                 P("gx", "gy", None, None))

time: 37.1 us -> 31.3 us (0.84)
  local copies, waits for them, and re-layouts: 9.43 us -> 2.8 us
  Pallas kernels: 26.7 us -> 27.7 us
    unnamed x9 -> x2, local copies, waits for them, and re-layouts: 7.55 us -> 2.8 us
    reshape x1 -> x0, local copies, waits for them, and re-layouts: 1.22 us -> none  [body(): cinv.reshape(ti, tj, kc * kc)]
    pallas_call x1, Pallas kernels: 26.7 us -> 27.7 us  [body(): pl.pallas_call(functools.partial(kernel, nx, ny, ti, tj, n, kc), out_shap...]
    pallas_call x1 -> x0, local copies, waits for them, and re-layouts: 0.65 us -> none  [body(): pl.pallas_call(functools.partial(kernel, nx, ny, ti, tj, n, kc), out_shap...]
where the time goes in v2:
time: 31.3 us; the launch traced here: 31.1 us
  Pallas kernels  27.7 us (88%)
  local copies, waits for them, and re-layouts  2.8 us (9%)
  between operations  0.64 us (2%)
    pallas_call x1, Pallas kernels, body(): pl.pallas_call(functools.partial(kernel, nx, ny, ti, tj, n, kc), out_shap...  27.7 us
    unnamed x2, local copies, waits for them, and re-layouts  2.8 us

profile of v2, /device:TPU:0, one launch (start us, length us, event | category | flops | bytes accessed | tf_op | source)
XLA Modules:
  0.0 31.1 jit_solution(3194566526482993286)
XLA Ops:
  0.6 27.7 %shard_map.77 = (f32[16,16,128]{2,1,0:T(8,128)}, f32[2,3]{1,0:T(2,128)}) custom-call(f32[16,16,128]{2,1,0:T(8,128)} %rhs_h.1, bf16[16,16,128,128]{3,2,1,0:T(8,128)(2,1)} %diag.1, bf16[4,128,128]{2,1,0:T(8,128)(2,1)} %lift_h.1, s32[16,4,16]{2,1,0:T(4,128)} %bitcast.7, f32[8,128]{1,0:T(8,128)} %bitcast.8, f32[16,64,16]{2,1,0:T(8,128)} %bitcast.6), custom_call_target="tpu_custom_call" | custom-call | tf_op jit(solution)/shard_map/pallas_call | solution.py:388
  28.3 1.6 %copy.10 = f32[16,16,128]{2,1,0:T(8,128)} copy(f32[16,16,128]{2,1,0:T(8,128)} %get-tuple-element.8) | data formatting | bytes 262144
  29.9 1.2 %copy.11 = f32[3,2]{0,1:T(2,128)} copy(f32[3,2]{0,1:T(2,128)} %bitcast.9) | data formatting | bytes 48

commit v3 on v2

--- a/solution.py
+++ b/solution.py
@@ -234,7 +234,7 @@
     def three_lines(g):
         return (line_sum(g, gx), line_sum(g, jnp.maximum(gx - 1, 0)), line_sum(g, jnp.minimum(gx + 1, nx - 1)))
 
-    def precondition(f_own, f_halo, lines):
+    def precondition(f_own, f_halo, lines, coarse):
         p_c, p_n, p_s = lines
         stack = jnp.concatenate([
             jnp.where(pick, jnp.broadcast_to(p_c, (ti, n)), 0.0),
@@ -242,7 +242,7 @@
             jnp.broadcast_to(jnp.where(lane1 // kc == 0, p_s, 0.0), (8, n))], axis=0)
         mean = hdot(stack, G) * (1.0 / (ny * tj))
         m_c, m_n, m_s = mean[0:ti], mean[ti:ti + 1], mean[ti + 8:ti + 9]
-        c_own = hdot(f_own, RE) - spread(m_c)
+        c_own = coarse - spread(m_c)
         c_halo = hdot(f_halo, RE)
         m_halo = jnp.concatenate([
             jnp.broadcast_to(m_n, (tj, n)), jnp.broadcast_to(m_s, (tj, n)), m_c, m_c, m_c, m_c,
@@ -294,6 +294,7 @@
             wbuf[q] += prod[0:tj, 0:n]
             wbuf[q + 1] += prod[tj:2 * tj, n:2 * n]
 
+    coarse_rhs = hdot(rhs2, RE)
     bc_wait(0, "recv")
     rim_wait(0, "recv")
     rim_wait(2, "recv")
@@ -306,7 +307,8 @@
     v1 = rhs2 * inv_len
     v1_halo = jnp.where(valid, halos[0] * inv_len, 0.0)
     lines1 = [p * inv_len for p in three_lines(0)]
-    z1, z1_rim = precondition(v1, v1_halo, lines1)
+    coarse1 = coarse_rhs * inv_len
+    z1, z1_rim = precondition(v1, v1_halo, lines1, coarse1)
     for c in dcopies:
         c.wait()
     operator(z1, z1_rim)
@@ -320,6 +322,7 @@
     msgs[1, me, 0:1] = message([dot_one, p_one, total(gap * gap), own_n1])
     msgs[1, me, 1:2] = packed_rowsum(wbuf[...])
     broadcast(1)
+    coarse_w = hdot(w1, RE)
     bc_wait(1, "recv")
     rim_wait(1, "recv")
 
@@ -331,7 +334,7 @@
     v2 = (w1 - h11 * v1) * inv21
     v2_halo = jnp.where(valid, (halos[1] - h11 * v1_halo) * inv21, 0.0)
     lines2 = [(pw - h11 * pv) * inv21 for pw, pv in zip(three_lines(1), lines1)]
-    z2, z2_rim = precondition(v2, v2_halo, lines2)
+    z2, z2_rim = precondition(v2, v2_halo, lines2, (coarse_w - h11 * coarse1) * inv21)
     operator(z2, z2_rim)
     w2 = wbuf[...].reshape(elems, n)
     alpha = safe_div(total(v1 * v2), own_n1)
@@ -371,6 +374,11 @@
     for g in range(3):
         bc_wait(g, "send")
         rim_wait(g, "send")
+
+
+def hand_on(sol_in, hess_in, sol_out, hess_out):
+    sol_out[...] = sol_in[...]
+    hess_out[...] = hess_in[...]
 
 
 def solution(mesh):
@@ -416,6 +424,13 @@
             compiler_params=pltpu.CompilerParams(collective_id=0, has_side_effects=True,
                                                  vmem_limit_bytes=60 * 1024 * 1024),
         )(rhs, diag, lift, sflat, basis.T, cflat)
+        sol, hess = pl.pallas_call(
+            hand_on,
+            out_shape=(jax.ShapeDtypeStruct(sol.shape, F32), jax.ShapeDtypeStruct(hess.shape, F32)),
+            in_specs=[vm, vm],
+            out_specs=(vm, vm),
+            compiler_params=pltpu.CompilerParams(vmem_limit_bytes=60 * 1024 * 1024),
+        )(sol, hess)
         return sol, hess.T
 
     in_specs = (P("gx", "gy", None), P("gx", "gy", None, None), P(), P("gx", "gy", None), P(),

time: 31.3 us -> 30 us (0.958)
  local copies, waits for them, and re-layouts: 2.8 us -> 0 us
  Pallas kernels: 27.7 us -> 29.2 us
    unnamed x2 -> x0, local copies, waits for them, and re-layouts: 2.8 us -> none
    pallas_call x0 -> x1, Pallas kernels: none -> 1.57 us  [body(): pl.pallas_call(hand_on, out_shape=(jax.ShapeDtypeStruct(sol.shape, F32),...]
where the time goes in v3:
time: 30 us; the launch traced here: 29.8 us
  Pallas kernels  29.2 us (97%)
  between operations  0.64 us (2%)
    pallas_call x1, Pallas kernels, body(): pl.pallas_call(functools.partial(kernel, nx, ny, ti, tj, n, kc), out_shap...  27.6 us
    pallas_call x1, Pallas kernels, body(): pl.pallas_call(hand_on, out_shape=(jax.ShapeDtypeStruct(sol.shape, F32),...  1.57 us

profile of v3, /device:TPU:0, one launch (start us, length us, event | category | flops | bytes accessed | tf_op | source)
XLA Modules:
  0.0 29.8 jit_solution(10490097318124667889)
XLA Ops:
  0.6 27.6 %shard_map.77 = (f32[16,16,128]{2,1,0:T(8,128)}, f32[2,3]{1,0:T(2,128)}) custom-call(f32[16,16,128]{2,1,0:T(8,128)} %rhs_h.1, bf16[16,16,128,128]{3,2,1,0:T(8,128)(2,1)} %diag.1, bf16[4,128,128]{2,1,0:T(8,128)(2,1)} %lift_h.1, s32[16,4,16]{2,1,0:T(4,128)} %bitcast.7, f32[8,128]{1,0:T(8,128)} %bitcast.8, f32[16,64,16]{2,1,0:T(8,128)} %bitcast.6), custom_call_target="tpu_custom_call" | custom-call | tf_op jit(solution)/shard_map/pallas_call | solution.py:396
  28.2 1.6 %shard_map.78 = (f32[16,16,128]{2,1,0:T(8,128)}, f32[2,3]{1,0:T(2,128)}) custom-call(f32[16,16,128]{2,1,0:T(8,128)} %get-tuple-element.6.sol_in, f32[2,3]{1,0:T(2,128)} %get-tuple-element.7.hess_in), custom_call_target="tpu_custom_call" | custom-call | tf_op jit(solution)/shard_map/pallas_call | solution.py:427

commit v4 on v3

--- a/solution.py
+++ b/solution.py
@@ -38,6 +38,15 @@
     elems = ti * tj
     kk = kc * kc
 
+    barrier = pltpu.get_barrier_semaphore()
+
+    def greet(k, carry):
+        t = lax.rem(me + k, count)
+        pl.semaphore_signal(barrier, inc=1, device_id=(t // ny, lax.rem(t, ny)), device_id_type=MESH)
+        return carry
+
+    lax.fori_loop(1, count, greet, 0)
+
     loads = [pltpu.make_async_copy(a, b, isem.at[q]) for q, (a, b) in enumerate(
         ((rhs_h, rhs), (basis_h, basis), (cinv_h, cinv), (state_h, state), (lift_h, lift)))]
     for c in loads:
@@ -45,15 +54,6 @@
     dcopies = [pltpu.make_async_copy(diag.at[q], dvm.at[q], dsem.at[q]) for q in range(ti)]
     for c in dcopies:
         c.start()
-
-    barrier = pltpu.get_barrier_semaphore()
-
-    def greet(k, carry):
-        t = lax.rem(me + k, count)
-        pl.semaphore_signal(barrier, inc=1, device_id=(t // ny, lax.rem(t, ny)), device_id_type=MESH)
-        return carry
-
-    lax.fori_loop(1, count, greet, 0)
 
     has_n, has_s, has_w, has_e = gx > 0, gx < nx - 1, gy > 0, gy < ny - 1
     h = 2 * ti + 2 * tj
@@ -172,9 +172,6 @@
     msgs[0, me, 0:1] = message([total(rhs2 * rhs2)])
     msgs[0, me, 1:2] = packed_rowsum(rhs3)
 
-    pl.semaphore_wait(barrier, count - 1)
-    broadcast(0)
-    start_all(rim_copies(0))
     loads[2].wait()
     cext[...] = jnp.zeros_like(cext)
     eye = (iota((tj, tj), 0) == iota((tj, tj), 1)).astype(F32)
@@ -185,6 +182,9 @@
     csend[tj:2 * tj] = c3d[ti - 1]
     csend[2 * tj:2 * tj + ti] = c3d[:, 0, :]
     csend[2 * tj + ti:2 * tj + 2 * ti] = c3d[:, tj - 1, :]
+    pl.semaphore_wait(barrier, count - 1)
+    broadcast(0)
+    start_all(rim_copies(0))
     start_all(coarse_copies())
 
     RE = hdot(Rt, e1, over_first)

time: 30 us -> 31.6 us (1.053)
  Pallas kernels: 29.2 us -> 30.8 us
    pallas_call x1, Pallas kernels: 27.6 us -> 29.2 us  [body(): pl.pallas_call(functools.partial(kernel, nx, ny, ti, tj, n, kc), out_shap...]
where the time goes in v4:
time: 31.6 us; the launch traced here: 31.5 us
  Pallas kernels  30.8 us (97%)
  between operations  0.64 us (2%)
    pallas_call x1, Pallas kernels, body(): pl.pallas_call(functools.partial(kernel, nx, ny, ti, tj, n, kc), out_shap...  29.2 us
    pallas_call x1, Pallas kernels, body(): pl.pallas_call(hand_on, out_shape=(jax.ShapeDtypeStruct(sol.shape, F32),...  1.57 us

profile of v4, /device:TPU:0, one launch (start us, length us, event | category | flops | bytes accessed | tf_op | source)
XLA Modules:
  0.0 31.5 jit_solution(6024592945825416066)
XLA Ops:
  0.6 29.2 %shard_map.77 = (f32[16,16,128]{2,1,0:T(8,128)}, f32[2,3]{1,0:T(2,128)}) custom-call(f32[16,16,128]{2,1,0:T(8,128)} %rhs_h.1, bf16[16,16,128,128]{3,2,1,0:T(8,128)(2,1)} %diag.1, bf16[4,128,128]{2,1,0:T(8,128)(2,1)} %lift_h.1, s32[16,4,16]{2,1,0:T(4,128)} %bitcast.7, f32[8,128]{1,0:T(8,128)} %bitcast.8, f32[16,64,16]{2,1,0:T(8,128)} %bitcast.6), custom_call_target="tpu_custom_call" | custom-call | tf_op jit(solution)/shard_map/pallas_call | solution.py:396
  29.9 1.6 %shard_map.78 = (f32[16,16,128]{2,1,0:T(8,128)}, f32[2,3]{1,0:T(2,128)}) custom-call(f32[16,16,128]{2,1,0:T(8,128)} %get-tuple-element.6.sol_in, f32[2,3]{1,0:T(2,128)} %get-tuple-element.7.hess_in), custom_call_target="tpu_custom_call" | custom-call | tf_op jit(solution)/shard_map/pallas_call | solution.py:427
